TPU v7x, 32 devices: a whole 2x2x4 slice. The times are simulated.
32 devices in a mesh: view: 4 (over x, core), pencil: 8 (over z, y).
Axes of the slice: x: 2, y: 2, z: 4, core: 2. Of those that a mesh axis runs over, the one named last changes fastest.
Arguments:
- recorded: float32 [4, 256, 256, 256], P('view', 'pencil'), may hold values from 0.5 to 4
- spectral_weight: float32 [4, 256, 256, 256], P('view', None, 'pencil'), may hold values from 0.05 to 1
- psf_taps: float32 [4, 3, 9], replicated, may hold values from 0.1 to 1
Outputs:
- joined_volume: float32 [256, 256, 256], P('pencil', 'view')
- estimate: float32 [256, 256, 256], P('pencil', 'view')
All inputs are finite; a program needn't handle non-finite values.
Results may differ from a plain program's by a relative error of at most 0.00029.
Values sent between devices are 32-bit elements; how exact they have to be, the bound alone decides.
No kernel may reach another device: no remote copies, remote signals or barrier semaphores. Data moves between devices by JAX's collectives and lax.ppermute only.
A program may use at most 192 MiB of HBM per device.

v0:
```python
import math

import jax
import jax.numpy as jnp
from jax import lax
from jax.sharding import PartitionSpec as P

NZ = 256
NY = 256
NX = 256
ITERS = 2


def padded_2(shard, sides, width):
    for axis, dim in sides:
        devices, length = (lax.axis_size(axis), shard.shape[dim])
        up = [(i, (i + 1) % devices) for i in range(devices - 1)]
        down = [(j, i) for i, j in up]
        last = lax.slice_in_dim(shard, length - width, length, axis=dim)
        leading = lax.slice_in_dim(shard, 0, width, axis=dim)
        before = lax.ppermute(last, axis, up)
        after = lax.ppermute(leading, axis, down)
        shard = jnp.concatenate([before, shard, after], axis=dim)
    return shard


def tables(length):
    positions = jnp.arange(length, dtype=jnp.int32)
    product = positions[:, None] * positions[None, :] % length
    phases = product.astype(jnp.float32) * (2.0 * math.pi / length)
    return (jnp.cos(phases), jnp.sin(phases))


def mix(form, left, right):
    return jnp.einsum(form, left, right, precision=lax.Precision.HIGHEST)


def depth_forward(pieces):
    real_part, imag_part = pieces
    cosine, sine_part = tables(real_part.shape[0])
    out_real = mix("zyx,zk->kyx", real_part, cosine) + mix("zyx,zk->kyx", imag_part, sine_part)
    out_imag = mix("zyx,zk->kyx", imag_part, cosine) - mix("zyx,zk->kyx", real_part, sine_part)
    return (out_real, out_imag)


def depth_inverse(real_part, imag_part):
    cosine, sine_part = tables(real_part.shape[0])
    out_real = mix("kyx,kz->zyx", real_part, cosine) - mix("kyx,kz->zyx", imag_part, sine_part)
    out_imag = mix("kyx,kz->zyx", real_part, sine_part) + mix("kyx,kz->zyx", imag_part, cosine)
    return (out_real, out_imag)


def rows_inverse(pieces):
    real_part, imag_part = pieces
    cosine, sine_part = tables(real_part.shape[1])
    out_real = mix("zkx,ky->zyx", real_part, cosine) - mix("zkx,ky->zyx", imag_part, sine_part)
    out_imag = mix("zkx,ky->zyx", real_part, sine_part) + mix("zkx,ky->zyx", imag_part, cosine)
    return (out_real, out_imag)


def columns_inverse(real_part, imag_part):
    cosine, sine_part = tables(real_part.shape[2])
    total = mix("zyk,kx->zyx", real_part, cosine) - mix("zyk,kx->zyx", imag_part, sine_part)
    return total / float(NZ * NY * NX)


def valid_conv(padded, column, axis_dim, length):
    running = column[0] * lax.slice_in_dim(padded, 0, length, axis=axis_dim)
    for offset in range(1, column.shape[0]):
        running = running + column[offset] * lax.slice_in_dim(
            padded, offset, offset + length, axis=axis_dim
        )
    return running


def padded_conv(field, column, axis_dim, margin):
    padding = [(0, 0)] * field.ndim
    padding[axis_dim] = (margin, margin)
    return valid_conv(jnp.pad(field, padding), column, axis_dim, field.shape[axis_dim])


def blur_views(padded, tap_rows, depth, rows_count, margin):
    field = valid_conv(padded, tap_rows[0], 1, depth)
    field = valid_conv(field, tap_rows[1], 2, rows_count)
    return padded_conv(field, tap_rows[2], 3, margin)


def body(recorded, spectral_weight, psf_taps):
    view_count = lax.axis_size("view")
    view_index = lax.axis_index("view")
    slab = recorded[0]
    cos_x, sin_x = tables(slab.shape[2])
    cos_y, sin_y = tables(slab.shape[1])
    first_real = mix("zyx,xk->zyk", slab, cos_x)
    first_imag = -mix("zyx,xk->zyk", slab, sin_x)
    second_real = mix("zyx,yk->zkx", first_real, cos_y) + mix("zyx,yk->zkx", first_imag, sin_y)
    second_imag = mix("zyx,yk->zkx", first_imag, cos_y) - mix("zyx,yk->zkx", first_real, sin_y)
    spec_real, spec_imag = depth_forward(
        (
            lax.all_to_all(second_real, "pencil", split_axis=1, concat_axis=0, tiled=True),
            lax.all_to_all(second_imag, "pencil", split_axis=1, concat_axis=0, tiled=True),
        )
    )
    weights = spectral_weight[0]
    weighted_real = spec_real * weights
    weighted_imag = spec_imag * weights
    quarter = slab.shape[1] // view_count
    start = view_index * quarter
    summed_real, summed_imag = lax.psum((weighted_real, weighted_imag), "view")
    inv_real, inv_imag = depth_inverse(summed_real, summed_imag)
    rows_real, rows_imag = rows_inverse(
        (
            lax.all_to_all(inv_real, "pencil", split_axis=0, concat_axis=1, tiled=True),
            lax.all_to_all(inv_imag, "pencil", split_axis=0, concat_axis=1, tiled=True),
        )
    )
    joined_full = columns_inverse(rows_real, rows_imag)
    joined_volume = lax.dynamic_slice_in_dim(joined_full, start, quarter, 1)
    kernels = psf_taps / jnp.sum(psf_taps, axis=-1, keepdims=True)
    margin = kernels.shape[-1] // 2
    stacked = lax.all_to_all(recorded, "view", split_axis=2, concat_axis=0, tiled=True)
    tap_rows = jnp.transpose(kernels, (1, 2, 0))[:, :, :, None, None, None]
    back_rows = tap_rows[:, ::-1]
    local = 0.1 + jax.nn.softplus(joined_volume)
    depth = local.shape[0]
    for repeat in range(ITERS):
        padded = padded_2(local, (("view", 1), ("pencil", 0)), margin)
        blurred = blur_views(padded[None], tap_rows, depth, quarter, margin)
        ratio = stacked / blurred
        padded_ratio = padded_2(ratio, (("view", 2), ("pencil", 1)), margin)
        correction = blur_views(padded_ratio, back_rows, depth, quarter, margin)
        local = local * jnp.sum(correction, axis=0) / view_count
    return (joined_volume, local)


def solution(mesh):
    return jax.shard_map(
        body,
        mesh=mesh,
        in_specs=(P("view", "pencil", None, None), P("view", None, "pencil", None), P()),
        out_specs=(P("pencil", "view", None), P("pencil", "view", None)),
        check_vma=False,
    )
```

profile of v0, /device:TPU:25, one launch (start us, length us, event | category | flops | bytes accessed | tf_op | source)
XLA Modules:
  0.0 1960.9 jit_solution(9329688927747642899)
XLA Ops:
  7.2 19.4 fusion.127
  26.6 15.0 fusion.129
  41.6 17.4 fusion.121
  59.1 18.3 add_bitcast_fusion
  77.4 8.1 copy.153
  85.5 6.0 all-to-all-start
  91.5 18.3 fusion.119
  109.7 18.0 subtract_bitcast_fusion
  127.7 11.5 copy.160
  139.2 134.6 %all-to-all-done = f32[32,256,256]{2,0,1:T(8,128)} async-done(((f32[32,256,256]{2,0,1:T(8,128)}), f32[32,256,256]{2,0,1:T(8,128)}, u32[]{:S(2)}, u32[]{:S(2)}) %all-to-all-start) | async-done | bytes 8388640 | tf_op jit(solution)/shard_map/all_to_all | solution.py:100
  273.7 4.9 all-to-all-start.1
  278.7 8.3 copy.154
  287.0 174.1 %all-to-all-done.1 = f32[32,256,256]{2,0,1:T(8,128)} async-done(((f32[32,256,256]{2,0,1:T(8,128)}), f32[32,256,256]{2,0,1:T(8,128)}, u32[]{:S(2)}, u32[]{:S(2)}) %all-to-all-start.1) | async-done | bytes 8388640 | tf_op jit(solution)/shard_map/all_to_all | solution.py:101
  461.1 8.4 copy.161
  469.5 14.1 fusion.167
  483.6 11.6 fusion.172
  495.2 20.9 %bitcast_multiply_fusion = f32[256,32,256]{2,0,1:T(8,128)} fusion(f32[256,32,256]{2,0,1:T(8,128)} %fusion.167, f32[1,256,32,256]{3,2,1,0:T(8,128)} %param.4, f32[256,32,256]{2,0,1:T(8,128)S(1)} %bitcast.175), kind=kOutput, calls=%fused_computation.211 | convolution fusion | flops 6447562752 | bytes 33554432 | tf_op jit(solution)/shard_map/zyx,zk->kyx/dot_general | solution.py:35
  516.1 24.1 %bitcast_multiply_fusion.1 = f32[256,32,256]{2,0,1:T(8,128)} fusion(f32[256,32,256]{2,0,1:T(8,128)} %fusion.172, f32[1,256,32,256]{3,2,1,0:T(8,128)} %param.4, f32[256,32,256]{2,0,1:T(8,128)} %bitcast.177), kind=kOutput, calls=%fused_computation.212 | convolution fusion | flops 6447562752 | bytes 33554432 | tf_op jit(solution)/shard_map/zyx,zk->kyx/dot_general | solution.py:35
  540.2 288.2 %all-reduce.7.cloned.1.call-done = (f32[256,32,256]{2,0,1:T(8,128)}, f32[256,32,256]{2,0,1:T(8,128)}) async-done(((f32[256,32,256]{2,0,1:T(8,128)}, f32[256,32,256]{2,0,1:T(8,128)}), (f32[256,32,256]{2,0,1:T(8,128)}, f32[256,32,256]{2,0,1:T(8,128)})) %all-reduce.7.cloned.1.call-update) | async-done | bytes 16777232 | tf_op jit(solution)/shard_map/psum | solution.py:109
  828.4 12.5 fusion.153
  840.9 12.2 convolution_add_fusion
  853.1 11.4 copy.173
  864.6 5.5 all-to-all-start.3
  870.1 12.2 fusion.174
  882.2 12.6 convolution_subtract_fusion
  894.8 8.1 copy.168
  902.9 149.6 %all-to-all-done.3 = f32[256,32,256]{2,1,0:T(8,128)} async-done(((f32[256,32,256]{2,1,0:T(8,128)}), f32[256,32,256]{2,1,0:T(8,128)}, u32[]{:S(2)}, u32[]{:S(2)}) %all-to-all-start.3) | async-done | bytes 8388640 | tf_op jit(solution)/shard_map/all_to_all | solution.py:114
  1052.4 4.9 all-to-all-start.2
  1057.3 11.4 copy.178
  1073.0 11.6 fusion.163
  1084.6 12.0 fusion.155
  1096.6 143.0 %all-to-all-done.2 = f32[256,32,256]{2,1,0:T(8,128)} async-done(((f32[256,32,256]{2,1,0:T(8,128)}), f32[256,32,256]{2,1,0:T(8,128)}, u32[]{:S(2)}, u32[]{:S(2)}) %all-to-all-start.2) | async-done | bytes 8388640 | tf_op jit(solution)/shard_map/all_to_all | solution.py:113
  1239.6 6.1 all-to-all-start.4
  1250.0 11.6 fusion.151
  1261.6 11.6 fusion.176
  1273.2 13.4 fusion.115
  1286.6 11.0 fusion.117
  1307.4 30.3 %collective-permute-done = f32[32,4,256]{2,1,0:T(4,128)S(1)} collective-permute-done((f32[32,4,256]{2,1,0:T(4,128)S(1)}, f32[32,4,256]{2,1,0:T(4,128)S(1)}, u32[]{:S(2)}, u32[]{:S(2)}) %collective-permute-start) | collective-permute-done | bytes 131104 | tf_op jit(solution)/shard_map/ppermute | solution.py:21
  1351.5 4.9 slice_bitcast_fusion.17
  1367.0 5.4 multiply_add_fusion.1
  1372.5 11.6 fusion.107
  1384.1 45.1 %fusion.26 = f32[4,32,64,256]{3,1,2,0:T(8,128)} fusion(f32[4,32,64,256]{3,1,2,0:T(8,128)} %bitcast.45, f32[4,32,64,256]{3,1,2,0:T(8,128)} %fusion.107, f32[4]{0:T(128)S(1)} %get-tuple-element.3, f32[4]{0:T(128)S(1)} %get-tuple-element.4, f32[4]{0:T(128)S(1)} %get-tuple-element.5, f32[4]{0:T(128)S(1)} %get-tuple-element.6, f32[4]{0:T(128)S(1)} %get-tuple-element.7, ...), kind=kLoop, calls=%fused_computation.82 | loop fusion | flops 37748736 | bytes 25165968 | tf_op jit(solution)/shard_map/div | solution.py:129
  1440.3 4.4 collective-permute-done.5
  1444.7 8.9 pad_maximum_fusion.2
  1462.6 18.2 collective-permute-done.6
  1480.8 25.4 %collective-permute-done.7 = f32[4,4,72,256]{3,1,2,0:T(4,128)S(1)} collective-permute-done((f32[4,4,72,256]{3,1,2,0:T(4,128)S(1)}, f32[4,4,72,256]{3,1,2,0:T(4,128)S(1)}, u32[]{:S(2)}, u32[]{:S(2)}) %collective-permute-start.7) | collective-permute-done | bytes 1179680 | tf_op jit(solution)/shard_map/ppermute | solution.py:22
  1506.1 16.5 maximum_maximum_fusion
  1522.7 41.0 %fusion.9 = f32[4,32,72,256]{3,1,2,0:T(8,128)} fusion(f32[4,36,72,256]{3,1,2,0:T(8,128)} %get-tuple-element.38, f32[4,36,72,256]{3,1,2,0:T(8,128)} %get-tuple-element.37, f32[4]{0:T(128)S(1)} %get-tuple-element.17, f32[4]{0:T(128)S(1)} %get-tuple-element.18, f32[4]{0:T(128)S(1)} %get-tuple-element.19, f32[4]{0:T(128)S(1)} %get-tuple-element.20, ...), kind=kLoop, calls=%fused_computation.54 | loop fusion | flops 44826624 | bytes 94371984 | tf_op jit(solution)/shard_map/add | solution.py:70
  1563.7 29.6 %fusion.99 = f32[4,32,64,256]{3,1,2,0:T(8,128)} fusion(f32[4,32,72,256]{3,1,2,0:T(8,128)} %fusion.9, f32[4]{0:T(128)S(1)} %get-tuple-element.10, f32[4]{0:T(128)S(1)} %get-tuple-element.11, f32[4]{0:T(128)S(1)} %get-tuple-element.12, f32[4]{0:T(128)S(1)} %get-tuple-element.13, f32[4]{0:T(128)S(1)} %get-tuple-element.14, f32[4]{0:T(128)S(1)} %get-tuple-element.15, ...), kind=kLoop, calls=%fused_computation.174 | loop fusion | flops 35651584 | bytes 83886224 | tf_op jit(solution)/shard_map/add | solution.py:70
  1593.3 42.4 %fusion.134 = f32[32,64,256]{2,0,1:T(8,128)} fusion(f32[4,32,64,256]{3,1,2,0:T(8,128)} %fusion.99, f32[4]{0:T(128)S(1)} %get-tuple-element.3, f32[4]{0:T(128)S(1)} %get-tuple-element.4, f32[4]{0:T(128)S(1)} %get-tuple-element.5, f32[4]{0:T(128)S(1)} %get-tuple-element.6, f32[4]{0:T(128)S(1)} %get-tuple-element.7, f32[4]{0:T(128)S(1)} %get-tuple-element.8, ...), kind=kLoop, calls=%fused_computation.230 | loop fusion | flops 37224448 | bytes 10485904 | tf_op jit(solution)/shard_map/reduce_sum | solution.py:132
  1657.8 6.4 collective-permute-done.11
  1664.6 5.2 slice_bitcast_fusion.8
  1681.9 6.6 multiply_add_fusion
  1688.5 11.6 fusion.91
  1700.1 45.1 %fusion.59 = f32[4,32,64,256]{3,1,2,0:T(8,128)} fusion(f32[4,32,64,256]{3,1,2,0:T(8,128)} %bitcast.45, f32[4,32,64,256]{3,1,2,0:T(8,128)} %fusion.91, f32[4]{0:T(128)S(1)} %get-tuple-element.3, f32[4]{0:T(128)S(1)} %get-tuple-element.4, f32[4]{0:T(128)S(1)} %get-tuple-element.5, f32[4]{0:T(128)S(1)} %get-tuple-element.6, f32[4]{0:T(128)S(1)} %get-tuple-element.7, ...), kind=kLoop, calls=%fused_computation.115 | loop fusion | flops 37748736 | bytes 25165968 | tf_op jit(solution)/shard_map/div | solution.py:129
  1754.5 4.4 collective-permute-done.13
  1758.9 8.9 pad_maximum_fusion.3
  1776.8 18.7 collective-permute-done.14
  1795.5 25.4 %collective-permute-done.15 = f32[4,4,72,256]{3,1,2,0:T(4,128)S(1)} collective-permute-done((f32[4,4,72,256]{3,1,2,0:T(4,128)S(1)}, f32[4,4,72,256]{3,1,2,0:T(4,128)S(1)}, u32[]{:S(2)}, u32[]{:S(2)}) %collective-permute-start.15) | collective-permute-done | bytes 1179680 | tf_op jit(solution)/shard_map/ppermute | solution.py:22
  1820.8 16.5 maximum_maximum_fusion.1
  1837.4 41.0 %fusion.1 = f32[4,32,72,256]{3,1,2,0:T(8,128)} fusion(f32[4,36,72,256]{3,1,2,0:T(8,128)} %get-tuple-element.34, f32[4,36,72,256]{3,1,2,0:T(8,128)} %get-tuple-element.33, f32[4]{0:T(128)S(1)} %get-tuple-element.17, f32[4]{0:T(128)S(1)} %get-tuple-element.18, f32[4]{0:T(128)S(1)} %get-tuple-element.19, f32[4]{0:T(128)S(1)} %get-tuple-element.20, ...), kind=kLoop, calls=%fused_computation.38 | loop fusion | flops 44826624 | bytes 94371984 | tf_op jit(solution)/shard_map/add | solution.py:70
  1878.4 29.6 %fusion.83 = f32[4,32,64,256]{3,1,2,0:T(8,128)} fusion(f32[4,32,72,256]{3,1,2,0:T(8,128)} %fusion.1, f32[4]{0:T(128)S(1)} %get-tuple-element.10, f32[4]{0:T(128)S(1)} %get-tuple-element.11, f32[4]{0:T(128)S(1)} %get-tuple-element.12, f32[4]{0:T(128)S(1)} %get-tuple-element.13, f32[4]{0:T(128)S(1)} %get-tuple-element.14, f32[4]{0:T(128)S(1)} %get-tuple-element.15, ...), kind=kLoop, calls=%fused_computation.140 | loop fusion | flops 35651584 | bytes 83886224 | tf_op jit(solution)/shard_map/add | solution.py:70
  1908.0 41.6 %fusion.133 = f32[32,64,256]{2,0,1:T(8,128)} fusion(f32[4,32,64,256]{3,1,2,0:T(8,128)} %fusion.83, f32[4]{0:T(128)S(1)} %get-tuple-element.3, f32[4]{0:T(128)S(1)} %get-tuple-element.4, f32[4]{0:T(128)S(1)} %get-tuple-element.5, f32[4]{0:T(128)S(1)} %get-tuple-element.6, f32[4]{0:T(128)S(1)} %get-tuple-element.7, f32[4]{0:T(128)S(1)} %get-tuple-element.8, ...), kind=kLoop, calls=%fused_computation.229 | loop fusion | flops 37224448 | bytes 10485904 | tf_op jit(solution)/shard_map/reduce_sum | solution.py:132
  1949.6 4.3 fusion.143
  (103 shorter events, 115.4 us)
Async XLA Ops:
  7.2 19.4 copy-start.2
  26.6 15.0 copy-start.3
  41.6 35.8 %copy-start = (f32[256,32,256]{2,0,1:T(8,128)}, f32[256,32,256]{2,0,1:T(8,128)S(1)}, u32[]{:S(2)}) copy-start(f32[256,32,256]{2,0,1:T(8,128)S(1)} %fusion.129) | copy-start | bytes 25165828
  85.5 188.2 %all-to-all-start = ((f32[32,256,256]{2,0,1:T(8,128)}), f32[32,256,256]{2,0,1:T(8,128)}, u32[]{:S(2)}, u32[]{:S(2)}) async-start(f32[32,256,256]{2,0,1:T(8,128)} %copy.153), calls=%async_computation | async-start | bytes 16777216 | tf_op jit(solution)/shard_map/all_to_all | solution.py:100
  91.5 18.3 copy-start.1
  273.7 187.3 %all-to-all-start.1 = ((f32[32,256,256]{2,0,1:T(8,128)}), f32[32,256,256]{2,0,1:T(8,128)}, u32[]{:S(2)}, u32[]{:S(2)}) async-start(f32[32,256,256]{2,0,1:T(8,128)} %copy.160), calls=%async_computation.1 | async-start | bytes 16777216 | tf_op jit(solution)/shard_map/all_to_all | solution.py:101
  278.7 549.7 %all-reduce.7.cloned.1.call-start = ((), (), s32[]{:S(2)}) async-start(), calls=%async_computation.5 | async-start | bytes 33554432 | tf_op jit(solution)/shard_map/psum | solution.py:109
  461.0 22.5 %slice-start = ((s8[8388608]{0:T(1024)(128)(4,1)}), s8[4194304]{0:T(1024)(128)(4,1)S(1)}, s32[]{:S(2)}) async-start(s8[8388608]{0:T(1024)(128)(4,1)} %bitcast.172), calls=%async_computation.6 | async-start | bytes 8388608
  469.5 14.1 slice-start.1
  828.4 12.5 copy-start.4
  864.6 187.8 %all-to-all-start.3 = ((f32[256,32,256]{2,1,0:T(8,128)}), f32[256,32,256]{2,1,0:T(8,128)}, u32[]{:S(2)}, u32[]{:S(2)}) async-start(f32[256,32,256]{2,1,0:T(8,128)} %copy.173), calls=%async_computation.3 | async-start | bytes 16777216 | tf_op jit(solution)/shard_map/all_to_all | solution.py:114
  1052.4 187.2 %all-to-all-start.2 = ((f32[256,32,256]{2,1,0:T(8,128)}), f32[256,32,256]{2,1,0:T(8,128)}, u32[]{:S(2)}, u32[]{:S(2)}) async-start(f32[256,32,256]{2,1,0:T(8,128)} %copy.168), calls=%async_computation.2 | async-start | bytes 16777216 | tf_op jit(solution)/shard_map/all_to_all | solution.py:113
  1239.6 144.5 %all-to-all-start.4 = ((f32[1,32,256,256]{3,1,0,2:T(8,128)}), f32[1,32,256,256]{3,1,0,2:T(8,128)}, u32[]{:S(2)}, u32[]{:S(2)}) async-start(f32[1,32,256,256]{3,1,0,2:T(8,128)} %copy.178), calls=%async_computation.4 | async-start | bytes 16777216 | tf_op jit(solution)/shard_map/all_to_all | solution.py:121
  1250.0 23.2 %slice-start.4 = ((s8[8388608]{0:T(1024)(128)(4,1)}), s8[4194304]{0:T(1024)(128)(4,1)S(1)}, s32[]{:S(2)}) async-start(s8[8388608]{0:T(1024)(128)(4,1)} %bitcast.180), calls=%async_computation.10 | async-start | bytes 8388608
  1261.6 11.6 slice-start.5
  1261.6 25.0 %slice-start.2 = ((s8[8388608]{0:T(1024)(128)(4,1)}), s8[4194304]{0:T(1024)(128)(4,1)S(1)}, s32[]{:S(2)}) async-start(s8[8388608]{0:T(1024)(128)(4,1)} %bitcast.178), calls=%async_computation.8 | async-start | bytes 8388608
  1273.2 13.4 slice-start.3
  1297.7 48.1 %copy-start.12 = (f32[4,3,9]{2,0,1:T(4,128)S(1)}, f32[4,3,9]{2,0,1:T(4,128)}, u32[]{:S(2)}) copy-start(f32[4,3,9]{2,0,1:T(4,128)} %param.5) | copy-start | bytes 1300
  1302.0 35.8 %collective-permute-start = (f32[32,4,256]{2,1,0:T(4,128)S(1)}, f32[32,4,256]{2,1,0:T(4,128)S(1)}, u32[]{:S(2)}, u32[]{:S(2)}) collective-permute-start(f32[32,4,256]{2,1,0:T(4,128)S(1)} %get-tuple-element.69), channel_id=1, source_target_pairs={{0,8},{8,16},{16,24},{1,9},{9,17},{17,25},{2,10},{10,18},{18,26},{... | collective-permute-start | bytes 393224 | tf_op jit(solution)/shard_map/ppermute | solution.py:21
  1305.5 34.0 %collective-permute-start.1 = (f32[32,4,256]{2,1,0:T(4,128)S(1)}, f32[32,4,256]{2,1,0:T(4,128)S(1)}, u32[]{:S(2)}, u32[]{:S(2)}) collective-permute-start(f32[32,4,256]{2,1,0:T(4,128)S(1)} %get-tuple-element.70), channel_id=1, source_target_pairs={{8,0},{16,8},{24,16},{9,1},{17,9},{25,17},{10,2},{18,10},{26,18},{... | collective-permute-start | bytes 393224 | tf_op jit(solution)/shard_map/ppermute | solution.py:22
  1339.6 8.5 collective-permute-start.2
  1341.8 9.3 collective-permute-start.3
  1356.4 5.2 copy-start.10
  1356.4 6.0 copy-start.8
  1356.4 6.8 copy-start.6
  1430.4 9.9 collective-permute-start.4
  1434.2 10.5 collective-permute-start.5
  1456.4 24.4 %collective-permute-start.6 = (f32[4,4,72,256]{3,1,2,0:T(4,128)S(1)}, f32[4,4,72,256]{3,1,2,0:T(4,128)S(1)}, u32[]{:S(2)}, u32[]{:S(2)}) collective-permute-start(f32[4,4,72,256]{3,1,2,0:T(4,128)S(1)} %get-tuple-element.39), channel_id=1, source_target_pairs={{0,1},{1,2},{2,3},{3,4},{4,5},{5,6},{6,7},{8,9},{9,10},{10,11},{11... | collective-permute-start | bytes 3538952 | tf_op jit(solution)/shard_map/ppermute | solution.py:21
  1458.3 47.8 %collective-permute-start.7 = (f32[4,4,72,256]{3,1,2,0:T(4,128)S(1)}, f32[4,4,72,256]{3,1,2,0:T(4,128)S(1)}, u32[]{:S(2)}, u32[]{:S(2)}) collective-permute-start(f32[4,4,72,256]{3,1,2,0:T(4,128)S(1)} %get-tuple-element.40), channel_id=1, source_target_pairs={{1,0},{2,1},{3,2},{4,3},{5,4},{6,5},{7,6},{9,8},{10,9},{11,10},{12... | collective-permute-start | bytes 3538952 | tf_op jit(solution)/shard_map/ppermute | solution.py:22
  1640.0 4.3 collective-permute-start.8
  1641.9 6.3 collective-permute-start.9
  1648.3 9.5 collective-permute-start.10
  1650.2 14.0 collective-permute-start.11
  1669.8 5.2 copy-start.11
  1669.8 6.0 copy-start.9
  1669.8 6.8 copy-start.7
  1672.4 5.0 copy-start.5
  1746.4 8.0 collective-permute-start.12
  1748.4 10.5 collective-permute-start.13
  1770.6 24.9 %collective-permute-start.14 = (f32[4,4,72,256]{3,1,2,0:T(4,128)S(1)}, f32[4,4,72,256]{3,1,2,0:T(4,128)S(1)}, u32[]{:S(2)}, u32[]{:S(2)}) collective-permute-start(f32[4,4,72,256]{3,1,2,0:T(4,128)S(1)} %get-tuple-element.35), channel_id=1, source_target_pairs={{0,1},{1,2},{2,3},{3,4},{4,5},{5,6},{6,7},{8,9},{9,10},{10,11},{11... | collective-permute-start | bytes 3538952 | tf_op jit(solution)/shard_map/ppermute | solution.py:21
  1772.5 48.3 %collective-permute-start.15 = (f32[4,4,72,256]{3,1,2,0:T(4,128)S(1)}, f32[4,4,72,256]{3,1,2,0:T(4,128)S(1)}, u32[]{:S(2)}, u32[]{:S(2)}) collective-permute-start(f32[4,4,72,256]{3,1,2,0:T(4,128)S(1)} %get-tuple-element.36), channel_id=1, source_target_pairs={{1,0},{2,1},{3,2},{4,3},{5,4},{6,5},{7,6},{9,8},{10,9},{11,10},{12... | collective-permute-start | bytes 3538952 | tf_op jit(solution)/shard_map/ppermute | solution.py:22
Sparse Core Ops, SparseCore 0:
  540.3 288.0 all-reduce.6
where the time goes:
time: 1970 us; the launch traced here: 1960 us
  waiting for transfers between devices  1040 us (53%)
  other arithmetic  415 us (21%)
  matrix products  298 us (15%)
  local copies, waits for them, and re-layouts  118 us (6%)
  starting transfers between devices  71.9 us (4%)
    dot_general x20, matrix products, mix(): return jnp.einsum(form, left, right, precision=lax.Precision.HIGHEST)  298 us
    psum x1, waiting for transfers between devices, body(): summed_real, summed_imag = lax.psum((weighted_real, weighted_imag), 'view')  288 us
    add x8, other arithmetic, valid_conv(): running + column[offset] * lax.slice_in_dim(padded, offset, offset + leng...  176 us
    all_to_all x1, waiting for transfers between devices, body(): lax.all_to_all(second_imag, 'pencil', split_axis=1, concat_axis=0, tiled=...  174 us
    all_to_all x1, waiting for transfers between devices, body(): lax.all_to_all(inv_imag, 'pencil', split_axis=0, concat_axis=1, tiled=True)  150 us
    all_to_all x1, waiting for transfers between devices, body(): lax.all_to_all(inv_real, 'pencil', split_axis=0, concat_axis=1, tiled=True)  143 us
    all_to_all x1, waiting for transfers between devices, body(): lax.all_to_all(second_real, 'pencil', split_axis=1, concat_axis=0, tiled=...  135 us
    div x2, other arithmetic, body(): ratio = stacked / blurred  90.1 us
  transfers between devices with their start and end apart: 22, of which 20 were waited for; matrix products, arithmetic and copies ran while one was open for 11% of the time, Pallas kernels for 0%

commit v1 on v0

v1 whole, which is shorter than its diff:
```python
import math

import jax
import jax.numpy as jnp
from jax import lax
from jax.experimental import pallas as pl
from jax.experimental.pallas import tpu as pltpu
from jax.sharding import PartitionSpec as P

ITERS = 2


def padded_2(shard, sides, width):
    for axis, dim in sides:
        devices, length = (lax.axis_size(axis), shard.shape[dim])
        before, after = ([], [])
        for hop in range(1, -(-width // length) + 1):
            take = min(length, width - (hop - 1) * length)
            up = [(i, i + hop) for i in range(devices - hop)]
            down = [(j, i) for i, j in up]
            last = lax.slice_in_dim(shard, length - take, length, axis=dim)
            leading = lax.slice_in_dim(shard, 0, take, axis=dim)
            before.insert(0, lax.ppermute(last, axis, up))
            after.append(lax.ppermute(leading, axis, down))
        shard = jnp.concatenate([*before, shard, *after], axis=dim)
    return shard


def tables(length):
    positions = jnp.arange(length, dtype=jnp.int32)
    product = positions[:, None] * positions[None, :] % length
    phases = product.astype(jnp.float32) * (2.0 * math.pi / length)
    return (jnp.cos(phases), jnp.sin(phases))


def mix(form, left, right):
    return jnp.einsum(form, left, right, precision=lax.Precision.HIGH)


def forward_matrix(length):
    c, s = tables(length)
    return jnp.stack([jnp.stack([c, s]), jnp.stack([-s, c])])


def inverse_matrix(length):
    c, s = tables(length)
    return jnp.stack([jnp.stack([c, -s]), jnp.stack([s, c])])


def row_forward(length):
    half = length // 2
    c, s = tables(length)
    imag = jnp.concatenate([c[:, half:half + 1], -s[:, 1:half]], axis=1)
    return jnp.stack([c[:, :half], imag])


def row_inverse(length, total):
    half = length // 2
    c, s = tables(length)
    real = jnp.concatenate([c[:1], 2.0 * c[1:half]], axis=0)
    imag = jnp.concatenate([c[half:half + 1], -2.0 * s[1:half]], axis=0)
    return jnp.stack([real, imag]) / float(total)


def mirrored(block, dim_z, dim_y):
    devices = lax.axis_size("pencil")
    n_z, n_y = (block.shape[dim_z], block.shape[dim_y])
    flipped = lax.rev(block, (dim_z, dim_y))
    flipped = jnp.concatenate(
        [
            lax.slice_in_dim(flipped, n_z - 1, n_z, axis=dim_z),
            lax.slice_in_dim(flipped, 0, n_z - 1, axis=dim_z),
        ],
        axis=dim_z,
    )
    far = lax.ppermute(
        lax.slice_in_dim(flipped, 0, n_y - 1, axis=dim_y),
        "pencil",
        [(i, devices - 1 - i) for i in range(devices)],
    )
    edge = lax.ppermute(
        lax.slice_in_dim(flipped, n_y - 1, n_y, axis=dim_y),
        "pencil",
        [(i, (devices - i) % devices) for i in range(devices)],
    )
    return jnp.concatenate([edge, far], axis=dim_y)


def halves(value):
    high = value.astype(jnp.bfloat16)
    low = (value - high.astype(jnp.float32)).astype(jnp.bfloat16)
    return high, low


def dot3(a, b):
    def one(u, w):
        return lax.dot_general(u, w, (((1,), (0,)), ((), ())), preferred_element_type=jnp.float32)

    return one(a[0], b[0]) + (one(a[0], b[1]) + one(a[1], b[0]))


def band(taps, outs, ins, offset):
    place = jnp.arange(ins)[None, :] - jnp.arange(outs)[:, None] + offset
    result = jnp.zeros((taps.shape[0], outs, ins), jnp.float32)
    for t in range(taps.shape[1]):
        result = result + jnp.where(place == t, 1.0, 0.0)[None] * taps[:, t][:, None, None]
    return result


def rl_step(padded, recorded, taps, mats, out_shape):
    views, depth1, rows1, width = recorded.shape
    depth, rows, _ = out_shape
    n_taps = taps.shape[2]
    margin = n_taps // 2
    rows2 = padded.shape[1]
    chunk = math.gcd(2 * margin, depth)

    def kernel(taps_ref, pad_ref, rec_ref, byh, byl, bxh, bxl, cyh, cyl, cxh, cxl, out_ref, ratio_ref):
        view = pl.program_id(0)

        def z_conv(ref, base, reverse):
            acc = None
            for t in range(n_taps):
                tap = taps_ref[view, 0, n_taps - 1 - t if reverse else t]
                term = tap * ref[pl.ds(base + t, chunk)]
                acc = term if acc is None else acc + term
            return acc

        def planes(value, x_high, x_low, y_high, y_low):
            n, r, w = value.shape
            flat = dot3(halves(value.reshape(n * r, w)), (x_high[0], x_low[0]))
            result = []
            for i in range(n):
                plane = halves(flat[i * r:(i + 1) * r])
                result.append(dot3((y_high[0], y_low[0]), plane))
            return result

        @pl.loop(0, depth1 // chunk)
        def _(c):
            base = c * chunk
            for i, blurred in enumerate(planes(z_conv(pad_ref, base, False), bxh, bxl, byh, byl)):
                ratio_ref[base + i] = rec_ref[0, base + i] / blurred

        @pl.loop(0, depth // chunk)
        def _(c):
            base = c * chunk
            for i, term in enumerate(planes(z_conv(ratio_ref, base, True), cxh, cxl, cyh, cyl)):
                @pl.when(view == 0)
                def _():
                    out_ref[base + i] = term

                @pl.when(view > 0)
                def _():
                    out_ref[base + i] = out_ref[base + i] + term

        @pl.when(view == views - 1)
        def _():
            @pl.loop(0, depth)
            def _(z):
                own = pad_ref[z + 2 * margin, 2 * margin:2 * margin + rows]
                out_ref[z] = own * out_ref[z] / views

    def per_view(array):
        return pl.BlockSpec((1,) + array.shape[1:], lambda v: (v,) + (0,) * (array.ndim - 1))

    return pl.pallas_call(
        kernel,
        grid=(views,),
        in_specs=[
            pl.BlockSpec(memory_space=pltpu.SMEM),
            pl.BlockSpec(padded.shape, lambda v: (0, 0, 0)),
            per_view(recorded),
        ] + [per_view(m) for m in mats],
        out_specs=pl.BlockSpec(out_shape, lambda v: (0, 0, 0)),
        out_shape=jax.ShapeDtypeStruct(out_shape, jnp.float32),
        scratch_shapes=[pltpu.VMEM((depth1, rows1, width), jnp.float32)],
        compiler_params=pltpu.CompilerParams(
            dimension_semantics=("arbitrary",), vmem_limit_bytes=60 * 1024 * 1024
        ),
    )(taps, padded, recorded, *mats)


def body(recorded, spectral_weight, psf_taps):
    views = lax.axis_size("view")
    pencils = lax.axis_size("pencil")
    slab = recorded[0]
    depth, n_y, n_x = slab.shape
    n_z = depth * pencils
    half = n_x // 2
    lines = n_y // pencils
    quarter = n_y // views

    weights = spectral_weight[0]
    columns = jnp.arange(n_x)
    turn = jnp.where(columns[:, None] == (n_x - columns[None, :half]) % n_x, 1.0, 0.0)
    turned = jnp.einsum("kqx,xh->kqh", weights, turn, precision=lax.Precision.HIGHEST)
    sym = 0.5 * (weights[:, :, :half] + mirrored(turned, 0, 1))
    nyquist = weights[:, :, half]
    sym_half = 0.5 * (nyquist + mirrored(nyquist, 0, 1))

    first = mix("zyx,dxh->zdyh", slab, row_forward(n_x))
    second = mix("cdqy,zdyh->qczh", forward_matrix(n_y), first)
    second = second.reshape(pencils, lines, 2, depth, half)
    second = lax.all_to_all(second, "pencil", split_axis=0, concat_axis=0, tiled=True)
    fz = forward_matrix(n_z).reshape(2, 2, n_z, pencils, depth)
    spec = mix("edkpz,pqdzh->qekh", fz, second)

    packed = spec[:, :, :, 0]
    other = mirrored(packed, 2, 0) * jnp.array([1.0, -1.0])[None, :, None]
    w_zero = sym[:, :, 0].T[:, None]
    w_half = sym_half.T[:, None]
    column = 0.5 * (packed * (w_zero + w_half) + other * (w_zero - w_half))
    weighted = spec * jnp.transpose(sym, (1, 0, 2))[:, None]
    lane = jnp.arange(half)
    weighted = jnp.where(lane == 0, column[..., None], weighted)
    summed = lax.psum_scatter(weighted, "view", scatter_dimension=0, tiled=True)

    iz = mix("dezk,qekh->zdqh", inverse_matrix(n_z), summed)
    own_z = n_z // (pencils * views)
    own_q = lines // views
    iz = iz.reshape(pencils * views, own_z, 2, own_q, half)
    iz = lax.all_to_all(iz, ("pencil", "view"), split_axis=0, concat_axis=0, tiled=True)
    my = inverse_matrix(n_y).reshape(2, 2, n_y, pencils * views, own_q)
    iy = mix("edysq,szdqh->zeyh", my, iz)
    thin = mix("zeyh,ehx->zyx", iy, row_inverse(n_x, n_z * n_y * n_x))
    joined_volume = lax.all_to_all(thin, "view", split_axis=1, concat_axis=0, tiled=True)

    kernels = psf_taps / jnp.sum(psf_taps, axis=-1, keepdims=True)
    margin = kernels.shape[-1] // 2
    sides = (("view", 1), ("pencil", 0))
    stacked = lax.all_to_all(recorded, "view", split_axis=2, concat_axis=0, tiled=True)
    stacked = padded_2(stacked, (("view", 2), ("pencil", 1)), margin)
    back = kernels[:, :, ::-1]
    mats = (
        *halves(band(kernels[:, 1], quarter + 2 * margin, quarter + 4 * margin, 0)),
        *halves(jnp.swapaxes(band(kernels[:, 2], n_x, n_x, margin), 1, 2)),
        *halves(band(back[:, 1], quarter, quarter + 2 * margin, 0)),
        *halves(jnp.swapaxes(band(back[:, 2], n_x, n_x, margin), 1, 2)),
    )
    local = 0.1 + jax.nn.softplus(joined_volume)
    for _ in range(ITERS):
        padded = padded_2(local, sides, 2 * margin)
        local = rl_step(padded, stacked, kernels, mats, local.shape)
    return (joined_volume, local)


def solution(mesh):
    return jax.shard_map(
        body,
        mesh=mesh,
        in_specs=(P("view", "pencil", None, None), P("view", None, "pencil", None), P()),
        out_specs=(P("pencil", "view", None), P("pencil", "view", None)),
        check_vma=False,
    )
```

time: 1970 us -> 965 us (0.49)
  waiting for transfers between devices: 1040 us -> 520 us
  other arithmetic: 415 us -> 58.9 us
  matrix products: 298 us -> 50.5 us
  Pallas kernels: 0 us -> 105 us
    all_to_all x4 -> x3, waiting for transfers between devices: 601 us -> 35.5 us  [the longest x1 35.5 us: body(): lax.all_to_all(iz, ('pencil', 'view'), split_axis=0, concat_axis=0, tiled...]
    psum x1 -> x0, waiting for transfers between devices: 288 us -> none  [body(): summed_real, summed_imag = lax.psum((weighted_real, weighted_imag), 'view')]
    dot_general x20 -> x7, matrix products: 298 us -> 50.5 us  [the longest x6 34.1 us: mix(): return jnp.einsum(form, left, right, precision=lax.Precision.HIGH)]
    ppermute x16 -> x18, waiting for transfers between devices: 154 us -> 338 us  [the longest x3 259 us: mirrored(): lax.ppermute(lax.slice_in_dim(flipped, n_y - 1, n_y, axis=dim_y), 'pencil...]
    add x8 -> x1, other arithmetic: 176 us -> 0.77 us  [body(): column = 0.5 * (packed * (w_zero + w_half) + other * (w_zero - w_half))]
    pallas_call x0 -> x2, Pallas kernels: none -> 105 us  [rl_step(): pl.pallas_call(kernel, grid=(views,), in_specs=[pl.BlockSpec(memory_space...]
    div x4 -> x0, other arithmetic: 98.6 us -> none  [the longest x2 90.1 us: body(): ratio = stacked / blurred]
    reduce_sum x2 -> x1, other arithmetic: 84 us -> 0.09 us  [body(): kernels = psf_taps / jnp.sum(psf_taps, axis=-1, keepdims=True)]
  transfers between devices with their start and end apart: 22 -> 23, of which waited for: 20 -> 13; matrix products, arithmetic and copies ran while one was open for 11% -> 19% of each run, Pallas kernels for 0% -> 0%
where the time goes in v1:
time: 965 us; the launch traced here: 948 us
  waiting for transfers between devices  520 us (54%)
  local copies, waits for them, and re-layouts  127 us (13%)
  Pallas kernels  105 us (11%)
  starting transfers between devices  70 us (7%)
  other arithmetic  58.9 us (6%)
  matrix products  50.5 us (5%)
  between operations  15.8 us (2%)
    ppermute x3, waiting for transfers between devices, mirrored(): lax.ppermute(lax.slice_in_dim(flipped, n_y - 1, n_y, axis=dim_y), 'pencil...  259 us
    pallas_call x2, Pallas kernels, rl_step(): pl.pallas_call(kernel, grid=(views,), in_specs=[pl.BlockSpec(memory_space...  105 us
    ppermute x6, waiting for transfers between devices, padded_2(): after.append(lax.ppermute(leading, axis, down))  75 us
    reduce_scatter x1, waiting for transfers between devices, body(): summed = lax.psum_scatter(weighted, 'view', scatter_dimension=0, tiled=True)  74.1 us
    all_to_all x1, waiting for transfers between devices, body(): lax.all_to_all(recorded, 'view', split_axis=2, concat_axis=0, tiled=True)  73.2 us
    unnamed x131, local copies, waits for them, and re-layouts  68.5 us
    all_to_all x1, waiting for transfers between devices, body(): lax.all_to_all(iz, ('pencil', 'view'), split_axis=0, concat_axis=0, tiled...  35.5 us
    dot_general x6, matrix products, mix(): return jnp.einsum(form, left, right, precision=lax.Precision.HIGH)  34.1 us
  transfers between devices with their start and end apart: 23, of which 13 were waited for; matrix products, arithmetic and copies ran while one was open for 19% of the time, Pallas kernels for 0%

profile of v1, /device:TPU:25, one launch (start us, length us, event | category | flops | bytes accessed | tf_op | source)
XLA Modules:
  0.0 948.4 jit_solution(16132812800767439927)
XLA Ops:
  11.2 6.4 fusion.4
  17.7 9.1 fusion.9
  26.8 10.5 %copy.25 = f32[256,2,32,128]{3,2,1,0:T(8,128)} copy(f32[256,2,32,128]{0,3,1,2:T(8,128)} %fusion.9) | data formatting | bytes 16777216 | tf_op jit(solution)/shard_map/cdqy,zdyh->qczh/transpose | solution.py:37
  37.2 5.5 all-to-all-start
  43.0 16.4 %fusion.12 = f32[256,32,128]{0,2,1:T(8,128)S(1)} fusion(f32[256,32,256]{2,1,0:T(8,128)} %bitcast.157, s32[128]{0:T(128)S(1)} %and_select_fusion), kind=kOutput, calls=%fused_computation.19 | convolution fusion | flops 3221291008 | bytes 12583424 | tf_op jit(solution)/shard_map/kqx,xh->kqh/dot_general | solution.py:196
  59.4 3.2 slice.346
  62.7 34.2 %reverse.8 = f32[256,32,128]{0,2,1:T(8,128)} reverse(f32[256,32,128]{0,2,1:T(8,128)} %bitcast.164), dimensions={0,1} | reverse | bytes 8388608
  96.9 5.5 slice.417
  102.3 11.6 %slice.263 = f32[1,32,128]{0,2,1:T(8,128)} reverse(f32[1,32,128]{0,2,1:T(8,128)S(1)} %slice-done), dimensions={0,1} | reverse | bytes 32768 | tf_op jit(solution)/shard_map/slice | solution.py:71
  113.9 6.0 pad_maximum_fusion.1
  121.1 3.1 collective-permute-start
  124.2 10.5 %copy.27 = f32[1,256,32,256]{1,2,3,0:T(8,128)} copy(f32[1,256,32,256]{3,2,1,0:T(8,128)} %param.5) | data formatting | bytes 16777216 | tf_op args[1]
  136.7 1.8 collective-permute-start.3
  138.6 2.3 collective-permute-start.2
  142.0 2.5 slice.344
  144.6 259.5 %collective-permute-done = f32[256,1,128]{0,2,1:T(8,128)S(1)} collective-permute-done((f32[256,1,128]{0,2,1:T(8,128)S(1)}, f32[256,1,128]{0,2,1:T(8,128)S(1)}, u32[]{:S(2)}, u32[]{:S(2)}) %collective-permute-start) | collective-permute-done | bytes 131104 | tf_op jit(solution)/shard_map/ppermute | solution.py:81
  404.0 4.9 fusion.8
  408.9 2.0 copy-done.7
  410.9 9.7 %fusion = f32[32,128,2,256,1,1]{3,1,4,0,2,5:T(8,128)S(1)} fusion(f32[8,32,2,32,128]{4,3,2,1,0:T(8,128)} %all-to-all-done, f32[1,1,256,8,32]{2,4,3,1,0:T(8,128)S(1)} %get-tuple-element.75, f32[1,1,256,8,32]{2,4,3,1,0:T(8,128)S(1)} %get-tuple-element.74, f32[1,1,256,8,32]{2,4,3,1,0:T(8,128)S(1)} %get-tuple-element.73), kind=kOutput, calls=%fused_computation.1 | convolution fusion | flops 6443237376 | bytes 17563648 | tf_op jit(solution)/shard_map/edkpz,pqdzh->qekh/dot_general | solution.py:37
  421.6 2.6 copy-done.2
  425.3 5.1 collective-permute-start.4
  431.4 10.2 %multiply_select_fusion = f32[32,2,256,128]{2,3,1,0:T(8,128)} fusion(f32[32,256,128]{1,2,0:T(8,128)} %bitcast.163, f32[32,2,256]{2,1,0:T(2,128)S(1)} %fusion.104, pred[128]{0:T(512)(128)(4,1)S(1)} %iota_compare_fusion.2, f32[32,128,2,256,1,1]{3,1,4,0,2,5:T(8,128)} %copy-done.2), kind=kLoop, calls=%fused_computation.11 | loop fusion | flops 4194304 | bytes 21037184 | tf_op jit(solution)/shard_map/jit(_where)/select_n | solution.py:215
  441.6 74.1 %reduce-scatter.2.cloned.1.call-done = f32[8,2,256,128]{2,3,1,0:T(8,128)} async-done(((f32[32,2,256,128]{2,3,1,0:T(8,128)}), f32[8,2,256,128]{2,3,1,0:T(8,128)}) %reduce-scatter.2.cloned.1.call-update) | async-done | bytes 2097168 | tf_op jit(solution)/shard_map/reduce_scatter | solution.py:216
  515.7 3.4 fusion.20
  519.2 2.0 copy.32
  521.1 5.3 all-to-all-start.1
  526.5 11.5 %copy.40 = f32[1,32,256,256]{3,1,0,2:T(8,128)} copy(f32[1,32,256,256]{3,2,1,0:T(8,128)} %param.4) | data formatting | bytes 16777216 | tf_op args[0]
  538.0 35.5 %all-to-all-done.1 = f32[32,8,2,8,128]{4,3,2,1,0:T(8,128)S(1)} async-done(((f32[32,8,2,8,128]{4,3,2,1,0:T(8,128)}), f32[32,8,2,8,128]{4,3,2,1,0:T(8,128)S(1)}, u32[]{:S(2)}, u32[]{:S(2)}) %all-to-all-start.1) | async-done | bytes 2097184 | tf_op jit(solution)/shard_map/all_to_all | solution.py:222
  573.4 6.0 all-to-all-start.3
  590.7 3.2 fusion.23
  593.9 2.2 copy.63
  596.2 2.4 convolution_bitcast_fusion
  598.5 73.2 %all-to-all-done.3 = f32[1,32,256,256]{3,1,0,2:T(8,128)} async-done(((f32[1,32,256,256]{3,1,0,2:T(8,128)}), f32[1,32,256,256]{3,1,0,2:T(8,128)}, u32[]{:S(2)}, u32[]{:S(2)}) %all-to-all-start.3) | async-done | bytes 8388640 | tf_op jit(solution)/shard_map/all_to_all | solution.py:231
  671.7 4.8 all-to-all-start.2
  679.0 1.8 copy.46
  680.8 1.8 copy.45
  682.6 1.8 copy.44
  684.4 1.8 copy.43
  688.2 8.3 copy.101
  696.8 1.9 collective-permute-start.11
  698.8 3.6 collective-permute-start.10
  702.6 1.7 subtract_convert_fusion.1
  704.3 1.7 subtract_convert_fusion
  708.5 1.8 pad_maximum_fusion.6
  710.3 1.9 collective-permute-start.13
  712.2 3.4 collective-permute-start.12
  717.1 2.3 copy.37
  720.7 2.3 collective-permute-start.7
  723.0 4.9 collective-permute-start.6
  731.4 2.6 collective-permute-start.9
  734.0 3.0 collective-permute-start.8
  737.9 41.6 %collective-permute-done.13 = f32[4,4,72,256]{3,2,1,0:T(8,128)S(1)} collective-permute-done((f32[4,4,72,256]{3,2,1,0:T(8,128)}, f32[4,4,72,256]{3,2,1,0:T(8,128)S(1)}, u32[]{:S(2)}, u32[]{:S(2)}) %collective-permute-start.13) | collective-permute-done | bytes 1179680 | tf_op jit(solution)/shard_map/ppermute | solution.py:24
  779.6 6.2 pad_maximum_fusion.rec_ref
  785.7 4.6 collective-permute-done.9
  790.3 2.3 pad_maximum_fusion.2.pad_ref
  792.6 52.7 %shard_map.59 = f32[32,64,256]{2,1,0:T(8,128)} custom-call(f32[4,3,9]{2,1,0:T(4,128)} %copy-done.36, f32[48,80,256]{2,1,0:T(8,128)} %pad_maximum_fusion.2.pad_ref, f32[4,40,72,256]{3,2,1,0:T(8,128)} %pad_maximum_fusion.rec_ref, bf16[4,72,80]{2,1,0:T(8,128)(2,1)} %get-tuple-element.45.byh, bf16[4,72,80]{2,1,0:T(8,128)(2,1)} %get-tuple-element.44.byl, ...), custom_call_target="tpu_custom_call" | custom-call | tf_op jit(solution)/shard_map/pallas_call | solution.py:166
  846.5 1.9 collective-permute-start.15
  848.4 3.6 collective-permute-start.14
  852.0 2.1 collective-permute-done.15
  856.7 2.8 collective-permute-start.17
  859.5 2.5 collective-permute-start.16
  862.0 24.1 %collective-permute-done.17 = f32[8,80,256]{2,1,0:T(8,128)S(1)} collective-permute-done((f32[8,80,256]{2,1,0:T(8,128)S(1)}, f32[8,80,256]{2,1,0:T(8,128)S(1)}, u32[]{:S(2)}, u32[]{:S(2)}) %collective-permute-start.17) | collective-permute-done | bytes 655392 | tf_op jit(solution)/shard_map/ppermute | solution.py:24
  886.2 2.3 pad_maximum_fusion.3.pad_ref
  888.4 52.7 %shard_map.60 = f32[32,64,256]{2,1,0:T(8,128)} custom-call(f32[4,3,9]{2,1,0:T(4,128)} %copy-done.36, f32[48,80,256]{2,1,0:T(8,128)} %pad_maximum_fusion.3.pad_ref, f32[4,40,72,256]{3,2,1,0:T(8,128)} %pad_maximum_fusion.rec_ref, bf16[4,72,80]{2,1,0:T(8,128)(2,1)} %get-tuple-element.45.byh, bf16[4,72,80]{2,1,0:T(8,128)(2,1)} %get-tuple-element.44.byl, ...), custom_call_target="tpu_custom_call" | custom-call | tf_op jit(solution)/shard_map/pallas_call | solution.py:166
  (223 shorter events, 40.6 us)
Async XLA Ops:
  37.2 373.7 %all-to-all-start = ((f32[8,32,2,32,128]{4,3,2,1,0:T(8,128)}), f32[8,32,2,32,128]{4,3,2,1,0:T(8,128)}, u32[]{:S(2)}, u32[]{:S(2)}) async-start(f32[8,32,2,32,128]{4,3,2,1,0:T(8,128)} %bitcast.158), calls=%async_computation | async-start | bytes 16777216 | tf_op jit(solution)/shard_map/all_to_all | solution.py:204
  42.7 473.0 %reduce-scatter.2.cloned.1.call-start = ((), (), s32[]{:S(2)}) async-start(), calls=%async_computation.5 | async-start | bytes 10485760 | tf_op jit(solution)/shard_map/reduce_scatter | solution.py:216
  119.9 284.2 %collective-permute-start.1 = (f32[256,31,128]{0,2,1:T(8,128)}, f32[256,31,128]{0,2,1:T(8,128)}, u32[]{:S(2)}, u32[]{:S(2)}) collective-permute-start(f32[256,31,128]{0,2,1:T(8,128)} %pad_maximum_fusion.1), channel_id=1, source_target_pairs={{0,7},{1,6},{2,5},{3,4},{4,3},{5,2},{6,1},{7,0},{8,15},{9,14},{10,... | collective-permute-start | bytes 12189704 | tf_op jit(solution)/shard_map/ppermute | solution.py:76
  121.1 282.9 %collective-permute-start = (f32[256,1,128]{0,2,1:T(8,128)S(1)}, f32[256,1,128]{0,2,1:T(8,128)S(1)}, u32[]{:S(2)}, u32[]{:S(2)}) collective-permute-start(f32[256,1,128]{0,2,1:T(8,128)S(1)} %pad_maximum_fusion.17), channel_id=1, source_target_pairs={{0,0},{1,7},{2,6},{3,5},{4,4},{5,3},{6,2},{7,1},{8,8},{9,15},{10,1... | collective-permute-start | bytes 393224 | tf_op jit(solution)/shard_map/ppermute | solution.py:81
  136.7 293.8 %collective-permute-start.3 = (f32[256,31]{0,1:T(8,128)S(1)}, f32[256,31]{0,1:T(8,128)S(1)}, u32[]{:S(2)}, u32[]{:S(2)}) collective-permute-start(f32[256,31]{0,1:T(8,128)S(1)} %pad_maximum_fusion.19), channel_id=1, source_target_pairs={{0,7},{1,6},{2,5},{3,4},{4,3},{5,2},{6,1},{7,0},{8,15},{9,14},{10,... | collective-permute-start | bytes 95240 | tf_op jit(solution)/shard_map/ppermute | solution.py:76
  138.6 291.8 %collective-permute-start.2 = (f32[256,1]{0,1:T(1,128)S(1)}, f32[256,1]{0,1:T(1,128)S(1)}, u32[]{:S(2)}, u32[]{:S(2)}) collective-permute-start(f32[256,1]{0,1:T(1,128)S(1)} %pad_maximum_fusion.21), channel_id=1, source_target_pairs={{0,0},{1,7},{2,6},{3,5},{4,4},{5,3},{6,2},{7,1},{8,8},{9,15},{10,1... | collective-permute-start | bytes 3080 | tf_op jit(solution)/shard_map/ppermute | solution.py:81
  425.3 5.9 collective-permute-start.5
  425.3 5.9 collective-permute-start.4
  521.1 52.3 %all-to-all-start.1 = ((f32[32,8,2,8,128]{4,3,2,1,0:T(8,128)}), f32[32,8,2,8,128]{4,3,2,1,0:T(8,128)S(1)}, u32[]{:S(2)}, u32[]{:S(2)}) async-start(f32[32,8,2,8,128]{4,3,2,1,0:T(8,128)} %bitcast.168), calls=%async_computation.2 | async-start | bytes 4194304 | tf_op jit(solution)/shard_map/all_to_all | solution.py:222
  538.0 41.5 %copy-start.37 = (f32[4,3,9]{2,0,1:T(4,128)S(1)}, f32[4,3,9]{2,0,1:T(4,128)}, u32[]{:S(2)}) copy-start(f32[4,3,9]{2,0,1:T(4,128)} %param.6) | copy-start | bytes 1300
  538.0 51.4 %copy-start.19 = (f32[256,256]{0,1:T(8,128)S(1)}, f32[256,256]{0,1:T(8,128)}, u32[]{:S(2)}) copy-start(f32[256,256]{0,1:T(8,128)} %copy-done.18) | copy-start | bytes 786436
  573.4 98.3 %all-to-all-start.3 = ((f32[1,32,256,256]{3,1,0,2:T(8,128)}), f32[1,32,256,256]{3,1,0,2:T(8,128)}, u32[]{:S(2)}, u32[]{:S(2)}) async-start(f32[1,32,256,256]{3,1,0,2:T(8,128)} %copy.40), calls=%async_computation.4 | async-start | bytes 16777216 | tf_op jit(solution)/shard_map/all_to_all | solution.py:231
  579.7 14.2 %copy-start.36 = (f32[4,3,9]{2,1,0:T(4,128)}, f32[4,3,9]{2,1,0:T(4,128)S(1)}, u32[]{:S(2)}) copy-start(f32[4,3,9]{2,1,0:T(4,128)S(1)} %copy_divide_fusion.taps_ref) | copy-start | bytes 1300
  596.2 81.2 %copy-start.20 = (f32[256,256]{0,1:T(8,128)S(1)}, f32[256,256]{0,1:T(8,128)}, u32[]{:S(2)}) copy-start(f32[256,256]{0,1:T(8,128)} %fusion.83) | copy-start | bytes 786436
  671.7 44.0 %all-to-all-start.2 = ((f32[8,256,256]{2,0,1:T(8,128)}), f32[8,256,256]{2,0,1:T(8,128)S(1)}, u32[]{:S(2)}, u32[]{:S(2)}) async-start(f32[8,256,256]{2,0,1:T(8,128)} %convolution_bitcast_fusion), calls=%async_computation.3 | async-start | bytes 4194304 | tf_op jit(solution)/shard_map/all_to_all | solution.py:226
  688.1 14.3 %copy-start.10 = (f32[256,256]{1,0:T(8,128)S(1)}, f32[256,256]{1,0:T(8,128)}, u32[]{:S(2)}) copy-start(f32[256,256]{1,0:T(8,128)} %copy.46) | copy-start | bytes 786436
  688.1 14.3 %copy-start.11 = (f32[256,256]{1,0:T(8,128)S(1)}, f32[256,256]{1,0:T(8,128)}, u32[]{:S(2)}) copy-start(f32[256,256]{1,0:T(8,128)} %copy.45) | copy-start | bytes 786436
  688.2 14.3 %copy-start.12 = (f32[256,256]{1,0:T(8,128)S(1)}, f32[256,256]{1,0:T(8,128)}, u32[]{:S(2)}) copy-start(f32[256,256]{1,0:T(8,128)} %copy.44) | copy-start | bytes 786436
  688.2 14.3 %copy-start.13 = (f32[256,256]{1,0:T(8,128)S(1)}, f32[256,256]{1,0:T(8,128)}, u32[]{:S(2)}) copy-start(f32[256,256]{1,0:T(8,128)} %copy.43) | copy-start | bytes 786436
  688.2 14.3 %copy-start.42 = (f32[4]{0:T(128)S(1)}, f32[4]{0:T(128)}, u32[]{:S(2)}) copy-start(f32[4]{0:T(128)} %get-tuple-element.20) | copy-start | bytes 52
  688.2 14.3 %copy-start.43 = (f32[4]{0:T(128)S(1)}, f32[4]{0:T(128)}, u32[]{:S(2)}) copy-start(f32[4]{0:T(128)} %get-tuple-element.21) | copy-start | bytes 52
  688.2 14.3 %copy-start.44 = (f32[4]{0:T(128)S(1)}, f32[4]{0:T(128)}, u32[]{:S(2)}) copy-start(f32[4]{0:T(128)} %get-tuple-element.22) | copy-start | bytes 52
  688.2 14.3 %copy-start.45 = (f32[4]{0:T(128)S(1)}, f32[4]{0:T(128)}, u32[]{:S(2)}) copy-start(f32[4]{0:T(128)} %get-tuple-element.23) | copy-start | bytes 52
  688.2 14.3 %copy-start.46 = (f32[4]{0:T(128)S(1)}, f32[4]{0:T(128)}, u32[]{:S(2)}) copy-start(f32[4]{0:T(128)} %get-tuple-element.24) | copy-start | bytes 52
  688.2 14.3 %copy-start.47 = (f32[4]{0:T(128)S(1)}, f32[4]{0:T(128)}, u32[]{:S(2)}) copy-start(f32[4]{0:T(128)} %get-tuple-element.25) | copy-start | bytes 52
  688.2 14.3 %copy-start.48 = (f32[4]{0:T(128)S(1)}, f32[4]{0:T(128)}, u32[]{:S(2)}) copy-start(f32[4]{0:T(128)} %get-tuple-element.26) | copy-start | bytes 52
  688.2 14.3 %copy-start.49 = (f32[4]{0:T(128)S(1)}, f32[4]{0:T(128)}, u32[]{:S(2)}) copy-start(f32[4]{0:T(128)} %get-tuple-element.27) | copy-start | bytes 52
  688.2 14.3 %copy-start.50 = (f32[4]{0:T(128)S(1)}, f32[4]{0:T(128)}, u32[]{:S(2)}) copy-start(f32[4]{0:T(128)} %get-tuple-element.28) | copy-start | bytes 52
  696.6 12.0 %copy-start = (f32[1,32,4,64,256]{4,3,1,2,0:T(8,128)}, f32[1,32,4,64,256]{4,3,1,2,0:T(8,128)S(1)}, u32[]{:S(2)}) copy-start(f32[1,32,4,64,256]{4,3,1,2,0:T(8,128)S(1)} %copy.101) | copy-start | bytes 25165828
  696.8 10.5 %collective-permute-start.11 = (f32[4,32,4,256]{3,2,1,0:T(4,128)S(1)}, f32[4,32,4,256]{3,2,1,0:T(4,128)S(1)}, u32[]{:S(2)}, u32[]{:S(2)}) collective-permute-start(f32[4,32,4,256]{3,2,1,0:T(4,128)S(1)} %get-tuple-element.51), channel_id=1, source_target_pairs={{8,0},{16,8},{24,16},{9,1},{17,9},{25,17},{10,2},{18,10},{26,18},{... | collective-permute-start | bytes 1572872 | tf_op jit(solution)/shard_map/ppermute | solution.py:24
  698.8 9.7 %collective-permute-start.10 = (f32[4,32,4,256]{3,2,1,0:T(4,128)S(1)}, f32[4,32,4,256]{3,2,1,0:T(4,128)S(1)}, u32[]{:S(2)}, u32[]{:S(2)}) collective-permute-start(f32[4,32,4,256]{3,2,1,0:T(4,128)S(1)} %get-tuple-element.50), channel_id=1, source_target_pairs={{0,8},{8,16},{16,24},{1,9},{9,17},{17,25},{2,10},{10,18},{18,26},{... | collective-permute-start | bytes 1572872 | tf_op jit(solution)/shard_map/ppermute | solution.py:23
  710.3 69.2 %collective-permute-start.13 = (f32[4,4,72,256]{3,2,1,0:T(8,128)}, f32[4,4,72,256]{3,2,1,0:T(8,128)S(1)}, u32[]{:S(2)}, u32[]{:S(2)}) collective-permute-start(f32[4,4,72,256]{3,2,1,0:T(8,128)} %get-tuple-element.47), channel_id=1, source_target_pairs={{1,0},{2,1},{3,2},{4,3},{5,4},{6,5},{7,6},{9,8},{10,9},{11,10},{12... | collective-permute-start | bytes 3538952 | tf_op jit(solution)/shard_map/ppermute | solution.py:24
  712.2 67.3 %collective-permute-start.12 = (f32[4,4,72,256]{3,2,1,0:T(8,128)}, f32[4,4,72,256]{3,2,1,0:T(8,128)}, u32[]{:S(2)}, u32[]{:S(2)}) collective-permute-start(f32[4,4,72,256]{3,2,1,0:T(8,128)} %get-tuple-element.46), channel_id=1, source_target_pairs={{0,1},{1,2},{2,3},{3,4},{4,5},{5,6},{6,7},{8,9},{9,10},{10,11},{11... | collective-permute-start | bytes 3538952 | tf_op jit(solution)/shard_map/ppermute | solution.py:23
  717.0 11.3 %copy-start.22 = (f32[72,80]{1,0:T(8,128)S(1)}, f32[72,80]{1,0:T(8,128)}, u32[]{:S(2)}) copy-start(f32[72,80]{1,0:T(8,128)} %get-tuple-element.87) | copy-start | bytes 69124
  717.0 11.3 %copy-start.23 = (f32[72,80]{1,0:T(8,128)S(1)}, f32[72,80]{1,0:T(8,128)}, u32[]{:S(2)}) copy-start(f32[72,80]{1,0:T(8,128)} %get-tuple-element.84) | copy-start | bytes 69124
  717.0 11.3 %copy-start.24 = (f32[72,80]{1,0:T(8,128)S(1)}, f32[72,80]{1,0:T(8,128)}, u32[]{:S(2)}) copy-start(f32[72,80]{1,0:T(8,128)} %get-tuple-element.85) | copy-start | bytes 69124
  717.0 11.3 %copy-start.25 = (f32[72,80]{1,0:T(8,128)S(1)}, f32[72,80]{1,0:T(8,128)}, u32[]{:S(2)}) copy-start(f32[72,80]{1,0:T(8,128)} %get-tuple-element.82) | copy-start | bytes 69124
  717.0 11.3 %copy-start.26 = (f32[72,80]{1,0:T(8,128)S(1)}, f32[72,80]{1,0:T(8,128)}, u32[]{:S(2)}) copy-start(f32[72,80]{1,0:T(8,128)} %get-tuple-element.83) | copy-start | bytes 69124
  717.0 11.3 %copy-start.38 = (f32[4]{0:T(128)S(1)}, f32[4]{0:T(128)}, u32[]{:S(2)}) copy-start(f32[4]{0:T(128)} %get-tuple-element.34) | copy-start | bytes 52
  717.0 11.3 %copy-start.39 = (f32[4]{0:T(128)S(1)}, f32[4]{0:T(128)}, u32[]{:S(2)}) copy-start(f32[4]{0:T(128)} %get-tuple-element.35) | copy-start | bytes 52
  717.0 11.3 %copy-start.40 = (f32[4]{0:T(128)S(1)}, f32[4]{0:T(128)}, u32[]{:S(2)}) copy-start(f32[4]{0:T(128)} %get-tuple-element.36) | copy-start | bytes 52
  717.1 11.3 %copy-start.41 = (f32[4]{0:T(128)S(1)}, f32[4]{0:T(128)}, u32[]{:S(2)}) copy-start(f32[4]{0:T(128)} %get-tuple-element.37) | copy-start | bytes 52
  719.3 12.0 %copy-start.8 = (f32[8,4,64,256]{3,2,0,1:T(8,128)}, f32[8,4,64,256]{3,2,0,1:T(8,128)S(1)}, u32[]{:S(2)}) copy-start(f32[8,4,64,256]{3,2,0,1:T(8,128)S(1)} %copy.37) | copy-start | bytes 6291460
  719.4 17.6 %copy-start.27 = (f32[64,72]{1,0:T(8,128)S(1)}, f32[64,72]{1,0:T(8,128)}, u32[]{:S(2)}) copy-start(f32[64,72]{1,0:T(8,128)} %fusion.144) | copy-start | bytes 55300
  719.4 17.6 %copy-start.28 = (f32[64,72]{1,0:T(8,128)S(1)}, f32[64,72]{1,0:T(8,128)}, u32[]{:S(2)}) copy-start(f32[64,72]{1,0:T(8,128)} %get-tuple-element.96) | copy-start | bytes 55300
  719.4 17.6 %copy-start.29 = (f32[64,72]{1,0:T(8,128)S(1)}, f32[64,72]{1,0:T(8,128)}, u32[]{:S(2)}) copy-start(f32[64,72]{1,0:T(8,128)} %get-tuple-element.97) | copy-start | bytes 55300
  719.4 17.6 %copy-start.30 = (f32[64,72]{1,0:T(8,128)S(1)}, f32[64,72]{1,0:T(8,128)}, u32[]{:S(2)}) copy-start(f32[64,72]{1,0:T(8,128)} %get-tuple-element.94) | copy-start | bytes 55300
  719.4 17.6 %copy-start.31 = (f32[64,72]{1,0:T(8,128)S(1)}, f32[64,72]{1,0:T(8,128)}, u32[]{:S(2)}) copy-start(f32[64,72]{1,0:T(8,128)} %get-tuple-element.95) | copy-start | bytes 55300
  719.4 17.6 %copy-start.32 = (f32[64,72]{1,0:T(8,128)S(1)}, f32[64,72]{1,0:T(8,128)}, u32[]{:S(2)}) copy-start(f32[64,72]{1,0:T(8,128)} %get-tuple-element.92) | copy-start | bytes 55300
  719.4 17.6 %copy-start.33 = (f32[64,72]{1,0:T(8,128)S(1)}, f32[64,72]{1,0:T(8,128)}, u32[]{:S(2)}) copy-start(f32[64,72]{1,0:T(8,128)} %get-tuple-element.93) | copy-start | bytes 55300
  719.4 17.6 %copy-start.34 = (f32[64,72]{1,0:T(8,128)S(1)}, f32[64,72]{1,0:T(8,128)}, u32[]{:S(2)}) copy-start(f32[64,72]{1,0:T(8,128)} %get-tuple-element.90) | copy-start | bytes 55300
  719.4 17.6 %copy-start.35 = (f32[64,72]{1,0:T(8,128)S(1)}, f32[64,72]{1,0:T(8,128)}, u32[]{:S(2)}) copy-start(f32[64,72]{1,0:T(8,128)} %get-tuple-element.91) | copy-start | bytes 55300
  719.4 60.1 %copy-start.1 = (f32[1,32,4,64,256]{4,3,1,2,0:T(8,128)S(1)}, f32[1,32,4,64,256]{4,3,1,2,0:T(8,128)}, u32[]{:S(2)}) copy-start(f32[1,32,4,64,256]{4,3,1,2,0:T(8,128)} %copy-done) | copy-start | bytes 25165828
  720.6 58.9 %copy-start.15 = (f32[4,32,4,256]{3,2,1,0:T(4,128)S(1)}, f32[4,32,4,256]{3,2,1,0:T(4,128)}, u32[]{:S(2)}) copy-start(f32[4,32,4,256]{3,2,1,0:T(4,128)} %copy-done.14) | copy-start | bytes 1572868
  720.6 58.9 %copy-start.17 = (f32[4,32,4,256]{3,2,1,0:T(4,128)S(1)}, f32[4,32,4,256]{3,2,1,0:T(4,128)}, u32[]{:S(2)}) copy-start(f32[4,32,4,256]{3,2,1,0:T(4,128)} %copy-done.16) | copy-start | bytes 1572868
  720.7 9.8 %collective-permute-start.7 = (f32[32,8,256]{2,1,0:T(8,128)S(1)}, f32[32,8,256]{2,1,0:T(8,128)S(1)}, u32[]{:S(2)}, u32[]{:S(2)}) collective-permute-start(f32[32,8,256]{2,1,0:T(8,128)S(1)} %get-tuple-element.59), channel_id=1, source_target_pairs={{8,0},{16,8},{24,16},{9,1},{17,9},{25,17},{10,2},{18,10},{26,18},{... | collective-permute-start | bytes 786440 | tf_op jit(solution)/shard_map/ppermute | solution.py:24
  723.0 8.3 collective-permute-start.6
  731.4 58.9 %collective-permute-start.9 = (f32[8,80,256]{2,1,0:T(8,128)S(1)}, f32[8,80,256]{2,1,0:T(8,128)S(1)}, u32[]{:S(2)}, u32[]{:S(2)}) collective-permute-start(f32[8,80,256]{2,1,0:T(8,128)S(1)} %get-tuple-element.55), channel_id=1, source_target_pairs={{1,0},{2,1},{3,2},{4,3},{5,4},{6,5},{7,6},{9,8},{10,9},{11,10},{12... | collective-permute-start | bytes 1966088 | tf_op jit(solution)/shard_map/ppermute | solution.py:24
  734.0 56.3 %collective-permute-start.8 = (f32[8,80,256]{2,1,0:T(8,128)S(1)}, f32[8,80,256]{2,1,0:T(8,128)S(1)}, u32[]{:S(2)}, u32[]{:S(2)}) collective-permute-start(f32[8,80,256]{2,1,0:T(8,128)S(1)} %get-tuple-element.54), channel_id=1, source_target_pairs={{0,1},{1,2},{2,3},{3,4},{4,5},{5,6},{6,7},{8,9},{9,10},{10,11},{11... | collective-permute-start | bytes 1966088 | tf_op jit(solution)/shard_map/ppermute | solution.py:23
  845.2 40.9 %copy-start.5 = (f32[32,64,256]{2,1,0:T(8,128)S(1)}, f32[32,64,256]{2,1,0:T(8,128)}, u32[]{:S(2)}) copy-start(f32[32,64,256]{2,1,0:T(8,128)} %shard_map.59) | copy-start | bytes 6291460
  846.5 7.7 collective-permute-start.15
  848.4 6.9 collective-permute-start.14
  856.7 29.5 %collective-permute-start.17 = (f32[8,80,256]{2,1,0:T(8,128)S(1)}, f32[8,80,256]{2,1,0:T(8,128)S(1)}, u32[]{:S(2)}, u32[]{:S(2)}) collective-permute-start(f32[8,80,256]{2,1,0:T(8,128)S(1)} %get-tuple-element.53), channel_id=1, source_target_pairs={{1,0},{2,1},{3,2},{4,3},{5,4},{6,5},{7,6},{9,8},{10,9},{11,10},{12... | collective-permute-start | bytes 1966088 | tf_op jit(solution)/shard_map/ppermute | solution.py:24
  859.5 26.7 %collective-permute-start.16 = (f32[8,80,256]{2,1,0:T(8,128)S(1)}, f32[8,80,256]{2,1,0:T(8,128)S(1)}, u32[]{:S(2)}, u32[]{:S(2)}) collective-permute-start(f32[8,80,256]{2,1,0:T(8,128)S(1)} %get-tuple-element.52), channel_id=1, source_target_pairs={{0,1},{1,2},{2,3},{3,4},{4,5},{5,6},{6,7},{8,9},{9,10},{10,11},{11... | collective-permute-start | bytes 1966088 | tf_op jit(solution)/shard_map/ppermute | solution.py:23
  (21 other events, 127.8 us)
Sparse Core Ops, SparseCore 0:
  441.7 73.9 reduce-scatter.1
